TPU v7x, 32 devices: a whole 2x2x4 slice. The times are simulated.
32 devices in a mesh: dp: 16 (over z, y, x), tensor: 2 (over core).
Axes of the slice: x: 2, y: 2, z: 4, core: 2. Of those that a mesh axis runs over, the one named last changes fastest.
Arguments:
- tokens: bfloat16 [32768, 768], P('dp'), may hold values from -6 to 6
- cotangent: bfloat16 [32768, 768], P('dp'), may hold values from -6 to 6
- seq_ids: int32 [32768], P('dp'), may hold values from 0 to 39, as said below
- block_slot: int32 [216], replicated, may hold values from 0 to 223, as said below
- masters: float32 [2, 224, 128, 128], P('tensor', 'dp')
- left_stats: float32 [2, 224, 128, 128], P('tensor', 'dp'), as said below
- right_stats: float32 [2, 224, 128, 128], P('tensor', 'dp'), as said below
- left_roots: float32 [2, 224, 128, 128], P('tensor', 'dp'), as said below
- right_roots: float32 [2, 224, 128, 128], P('tensor', 'dp'), as said below
- vectors: float32 [9984], replicated
- vector_momentum: float32 [9984], replicated, may hold values from -0.9 to 0.9
Outputs:
- mixed: bfloat16 [32768, 768], P(('dp', 'tensor'))
- input_grad: float32 [32768, 768], P(('dp', 'tensor'))
- matrix_grads: float32 [2, 224, 128, 128], P('tensor', 'dp')
- new_masters: float32 [2, 224, 128, 128], P('tensor', 'dp')
- new_left: float32 [2, 224, 128, 128], P('tensor', 'dp')
- new_right: float32 [2, 224, 128, 128], P('tensor', 'dp')
- new_vectors: float32 [9984], replicated
- new_vector_momentum: float32 [9984], replicated
Inputs may be any that keep to these rules, and one draw needn't show every extreme that they name: `seq_ids`: each aligned block of 2048 tokens holds either one sequence or 4 sequences of 512 tokens, half of the blocks of each kind; ids count the sequences in order from 0 and are equal within a sequence. `block_slot`: Distinct; slot s belongs to index s // 14 of dp; slots that no block names hold no block. `left_stats`: symmetric in each slot. `right_stats`: symmetric in each slot. `left_roots`: symmetric in each slot. `right_roots`: symmetric in each slot.
All inputs are finite; a program needn't handle non-finite values.
Results may differ from a plain program's by a relative error of at most 0.0095.
Values may be sent and summed in bfloat16 or wider, within the bound.
No kernel may reach another device: no remote copies, remote signals or barrier semaphores. Data moves between devices by JAX's collectives and lax.ppermute only.
A program may use at most 256 MiB of HBM per device.

v0:
```python
import jax
import jax.numpy as jnp
from jax import lax
from jax.sharding import PartitionSpec as P

H = 12
HD = 64
ROT = 16
FF = 3072
norm_eps = 1e-05
floor_score = -1e30
rate_matrix = 0.03
rate_vector = 1.5
decay_vector = 0.9


def contract(first_op, second_op, first_dim, second_dim):
    return lax.dot_general(
        first_op,
        second_op,
        (((first_dim,), (second_dim,)), ((), ())),
        preferred_element_type=jnp.float32,
    )


def unblock(blocks, row_total, col_total):
    blk_size = blocks.shape[-1]
    return (
        blocks.reshape(row_total // blk_size, col_total // blk_size, blk_size, blk_size)
        .transpose(0, 2, 1, 3)
        .reshape(row_total, col_total)
    )


def to_blocks(matrix, blk_size):
    row_count, col_count = matrix.shape
    return (
        matrix.reshape(row_count // blk_size, blk_size, col_count // blk_size, blk_size)
        .transpose(0, 2, 1, 3)
        .reshape(-1, blk_size, blk_size)
    )


def rotate(values, cosine_tab, sine_tab, local_heads):
    tok_rows = values.shape[0]
    shaped = values.reshape(tok_rows, local_heads, HD)
    rot_half = ROT // 2
    lower_half = shaped[:, :, :rot_half]
    upper_half = shaped[:, :, rot_half:ROT]
    turned = jnp.concatenate(
        [
            lower_half * cosine_tab - upper_half * sine_tab,
            upper_half * cosine_tab + lower_half * sine_tab,
            shaped[:, :, ROT:],
        ],
        axis=2,
    )
    return turned.reshape(tok_rows, local_heads * HD)


def slice_rows(array, row_start, row_count):
    return lax.dynamic_slice_in_dim(array, row_start, row_count, 0)


def back_norm(gradient, gain_vec, normed_rows, inv_rows):
    scaled = gradient * gain_vec
    centered = scaled - jnp.mean(scaled, axis=1, keepdims=True)
    return inv_rows * (
        centered - normed_rows * jnp.mean(scaled * normed_rows, axis=1, keepdims=True)
    )


def on_device(
    tokens,
    cotangent,
    seq_ids,
    block_slot,
    masters,
    left_stats,
    right_stats,
    left_roots,
    right_roots,
    vectors,
    vector_momentum,
):
    tensor_ways = lax.axis_size("tensor")
    tensor_index = lax.axis_index("tensor")
    data_ways = lax.axis_size("dp")
    data_index = lax.axis_index("dp")
    tok_rows, model_width = tokens.shape
    blk_size = masters.shape[-1]
    slot_count = masters.shape[1]
    local_heads = H // tensor_ways
    width_qkv = 3 * model_width // tensor_ways
    width_heads = model_width // tensor_ways
    width_hidden = FF // tensor_ways
    blocks_qkv = model_width // blk_size * (width_qkv // blk_size)
    blocks_attn = width_heads // blk_size * (model_width // blk_size)
    blocks_in = model_width // blk_size * (width_hidden // blk_size)
    mark_two = blocks_qkv + blocks_attn
    mark_three = mark_two + blocks_in
    copies = masters[0].astype(jnp.bfloat16)
    gathered = lax.all_gather(copies, "dp", axis=0, tiled=True)
    picked = jnp.take(gathered, block_slot, axis=0)
    w_qkv = unblock(picked[:blocks_qkv], model_width, width_qkv)
    w_attn = unblock(picked[blocks_qkv:mark_two], width_heads, model_width)
    w_in = unblock(picked[mark_two:mark_three], model_width, width_hidden)
    w_out = unblock(picked[mark_three:], width_hidden, model_width)
    gain_one = vectors[0:model_width]
    bias_one = vectors[model_width : 2 * model_width]
    gain_two = vectors[2 * model_width : 3 * model_width]
    bias_two = vectors[3 * model_width : 4 * model_width]
    bias_qkv = lax.dynamic_slice_in_dim(
        vectors, 4 * model_width + tensor_index * width_qkv, width_qkv
    )
    bias_attn = vectors[7 * model_width : 8 * model_width]
    bias_in = lax.dynamic_slice_in_dim(
        vectors, 8 * model_width + tensor_index * width_hidden, width_hidden
    )
    bias_out = vectors[8 * model_width + FF : 9 * model_width + FF]
    places = jnp.arange(tok_rows, dtype=jnp.int32)
    seq_first = jnp.concatenate([places[:1] == 0, seq_ids[1:] != seq_ids[:-1]])
    seq_start = lax.cummax(jnp.where(seq_first, places, 0), axis=0)
    position = (places - seq_start).astype(jnp.float32)
    rot_half = ROT // 2
    inverse = 10000.0 ** (-(2.0 * jnp.arange(rot_half, dtype=jnp.float32)) / ROT)
    angles = position[:, None] * inverse[None, :]
    cosine_tab = jnp.cos(angles)[:, None, :]
    sine_tab = jnp.sin(angles)[:, None, :]
    tokens_f = tokens.astype(jnp.float32)
    row_mean = jnp.mean(tokens_f, axis=1, keepdims=True)
    centered = tokens_f - row_mean
    inv_std = lax.rsqrt(jnp.mean(centered * centered, axis=1, keepdims=True) + norm_eps)
    normed = centered * inv_std
    norm_one = (normed * gain_one + bias_one).astype(jnp.bfloat16)
    norm_two = (normed * gain_two + bias_two).astype(jnp.bfloat16)
    mixed_qkv = jnp.dot(norm_one, w_qkv, preferred_element_type=jnp.float32) + bias_qkv
    queries = (
        rotate(mixed_qkv[:, :width_heads], cosine_tab, sine_tab, local_heads)
        .astype(jnp.bfloat16)
        .reshape(tok_rows, local_heads, HD)
    )
    keys_rot = (
        rotate(mixed_qkv[:, width_heads : 2 * width_heads], cosine_tab, sine_tab, local_heads)
        .astype(jnp.bfloat16)
        .reshape(tok_rows, local_heads, HD)
    )
    values_all = (
        mixed_qkv[:, 2 * width_heads :].astype(jnp.bfloat16).reshape(tok_rows, local_heads, HD)
    )
    blk_rows = min(512, tok_rows)
    block_total = tok_rows // blk_rows
    score_scale = HD ** (-0.5)

    def block_scores(block_index):
        row_low = block_index * blk_rows
        row_high = row_low + blk_rows
        scores = (
            jnp.einsum(
                "qhe,khe->hqk",
                queries[row_low:row_high],
                keys_rot[:row_high],
                preferred_element_type=jnp.float32,
            )
            * score_scale
        )
        allowed = (seq_ids[row_low:row_high, None] == seq_ids[None, :row_high]) & (
            places[row_low:row_high, None] >= places[None, :row_high]
        )
        return jnp.where(allowed[None], scores, floor_score)

    outputs = []
    log_sums = []
    for block_index in range(block_total):
        key_span = (block_index + 1) * blk_rows
        scores = block_scores(block_index)
        row_max = jnp.max(scores, axis=2, keepdims=True)
        exp_scores = jnp.exp(scores - row_max)
        row_total = jnp.sum(exp_scores, axis=2, keepdims=True)
        weights_low = (exp_scores / row_total).astype(jnp.bfloat16)
        outputs.append(
            jnp.einsum(
                "hqk,khe->qhe",
                weights_low,
                values_all[:key_span],
                preferred_element_type=jnp.float32,
            )
        )
        log_sums.append(row_max + jnp.log(row_total))
    attended = jnp.concatenate(outputs, axis=0).reshape(tok_rows, width_heads).astype(jnp.bfloat16)
    pre_hidden = jnp.dot(norm_two, w_in, preferred_element_type=jnp.float32) + bias_in
    hidden = jax.nn.gelu(pre_hidden, approximate=False).astype(jnp.bfloat16)
    own_rows = tok_rows // tensor_ways
    row_base = tensor_index * own_rows
    row_start = jnp.int32(0)
    attn_part = slice_rows(attended, row_start, lax.axis_size("tensor") * own_rows)
    hidden_part = slice_rows(hidden, row_start, lax.axis_size("tensor") * own_rows)
    branch_total = lax.psum_scatter(
        (
            jnp.dot(attn_part, w_attn, preferred_element_type=jnp.float32)
            + jnp.dot(hidden_part, w_out, preferred_element_type=jnp.float32)
        ).astype(jnp.bfloat16),
        "tensor",
        scatter_dimension=0,
        tiled=True,
    ).astype(jnp.float32)
    tokens_own = slice_rows(tokens_f, row_base, own_rows)
    mixed = (tokens_own + branch_total + bias_attn + bias_out).astype(jnp.bfloat16)
    grad_out_w = contract(hidden, cotangent, 0, 0)
    grad_hidden = contract(cotangent, w_out, 1, 1)
    density = jnp.exp(-0.5 * pre_hidden * pre_hidden) * 0.3989422804014327
    slope = 0.5 * (1.0 + lax.erf(pre_hidden * 0.7071067811865476)) + pre_hidden * density
    grad_pre = (grad_hidden * slope).astype(jnp.bfloat16)
    grad_in_w = contract(norm_two, grad_pre, 0, 0)
    grad_norm_two = contract(grad_pre, w_in, 1, 1)
    grad_bias_in = jnp.sum(grad_pre.astype(jnp.float32), axis=0)
    grad_attn_w = contract(attended, cotangent, 0, 0)
    grad_attended = (
        contract(cotangent, w_attn, 1, 1).astype(jnp.bfloat16).reshape(tok_rows, local_heads, HD)
    )
    grad_queries = []
    grad_keys = jnp.zeros((tok_rows, local_heads, HD), jnp.float32)
    grad_values = jnp.zeros((tok_rows, local_heads, HD), jnp.float32)
    for block_index in range(block_total):
        row_low = block_index * blk_rows
        row_high = row_low + blk_rows
        scores = block_scores(block_index)
        prob_full = jnp.exp(scores - log_sums[block_index])
        prob_low = prob_full.astype(jnp.bfloat16)
        grad_probs = jnp.einsum(
            "qhe,khe->hqk",
            grad_attended[row_low:row_high],
            values_all[:row_high],
            preferred_element_type=jnp.float32,
        )
        row_delta = jnp.sum(prob_full * grad_probs, axis=2, keepdims=True)
        grad_scores = (prob_full * (grad_probs - row_delta)).astype(jnp.bfloat16)
        grad_queries.append(
            jnp.einsum(
                "hqk,khe->qhe", grad_scores, keys_rot[:row_high], preferred_element_type=jnp.float32
            )
            * score_scale
        )
        grad_keys = grad_keys.at[:row_high].add(
            jnp.einsum(
                "hqk,qhe->khe",
                grad_scores,
                queries[row_low:row_high],
                preferred_element_type=jnp.float32,
            )
            * score_scale
        )
        grad_values = grad_values.at[:row_high].add(
            jnp.einsum(
                "hqk,qhe->khe",
                prob_low,
                grad_attended[row_low:row_high],
                preferred_element_type=jnp.float32,
            )
        )
    grad_query_all = jnp.concatenate(grad_queries, axis=0).reshape(tok_rows, width_heads)
    grad_mixed = jnp.concatenate(
        [
            rotate(grad_query_all, cosine_tab, -sine_tab, local_heads),
            rotate(grad_keys.reshape(tok_rows, width_heads), cosine_tab, -sine_tab, local_heads),
            grad_values.reshape(tok_rows, width_heads),
        ],
        axis=1,
    ).astype(jnp.bfloat16)
    grad_qkv_w = contract(norm_one, grad_mixed, 0, 0)
    grad_norm_one = contract(grad_mixed, w_qkv, 1, 1)
    grad_bias_qkv = jnp.sum(grad_mixed.astype(jnp.float32), axis=0)
    row_start = jnp.int32(0)
    row_count = lax.axis_size("tensor") * own_rows
    normed_rows = slice_rows(normed, row_start, row_count)
    inv_rows = slice_rows(inv_std, row_start, row_count)
    input_part = lax.psum_scatter(
        (
            back_norm(
                slice_rows(grad_norm_one, row_start, row_count), gain_one, normed_rows, inv_rows
            )
            + back_norm(
                slice_rows(grad_norm_two, row_start, row_count), gain_two, normed_rows, inv_rows
            )
        ).astype(jnp.bfloat16),
        "tensor",
        scatter_dimension=0,
        tiled=True,
    ).astype(jnp.float32)
    cot_own = slice_rows(cotangent, row_base, own_rows).astype(jnp.float32)
    input_grad = cot_own + input_part
    bias_grad_out = jnp.sum(cot_own, axis=0)
    pieces = [
        jnp.sum(grad_norm_one * normed, axis=0),
        jnp.sum(grad_norm_one, axis=0),
        jnp.sum(grad_norm_two * normed, axis=0),
        jnp.sum(grad_norm_two, axis=0),
        lax.dynamic_update_slice_in_dim(
            jnp.zeros((3 * model_width,), jnp.float32), grad_bias_qkv, tensor_index * width_qkv, 0
        ),
        bias_grad_out,
        lax.dynamic_update_slice_in_dim(
            jnp.zeros((FF,), jnp.float32), grad_bias_in, tensor_index * width_hidden, 0
        ),
        bias_grad_out,
    ]
    vector_sum = lax.psum(jnp.concatenate(pieces), ("dp", "tensor"))
    grad_scale = 1.0 / jnp.sqrt(jnp.float32(data_ways * tok_rows))
    vector_grad = vector_sum * grad_scale
    new_momentum = decay_vector * vector_momentum + (1.0 - decay_vector) * vector_grad
    new_vectors = vectors - rate_vector * new_momentum
    local_blocks = jnp.concatenate(
        [
            to_blocks(grad_qkv_w, blk_size),
            to_blocks(grad_attn_w, blk_size),
            to_blocks(grad_in_w, blk_size),
            to_blocks(grad_out_w, blk_size),
        ],
        axis=0,
    )
    slot_total = data_ways * slot_count
    summed = lax.psum(local_blocks, "dp")
    owner_of = (
        jnp.full((slot_total,), -1, jnp.int32)
        .at[block_slot]
        .set(jnp.arange(block_slot.shape[0], dtype=jnp.int32))
    )
    mine_blocks = lax.dynamic_slice_in_dim(owner_of, data_index * slot_count, slot_count, 0)
    owned = jnp.where(
        (mine_blocks >= 0)[:, None, None],
        jnp.take(summed, jnp.maximum(mine_blocks, 0), axis=0),
        0.0,
    )
    grad_blocks = owned * grad_scale
    highest = lax.Precision.HIGHEST
    new_left = (
        0.5 * left_stats[0]
        + 0.5 * jnp.einsum("sij,skj->sik", grad_blocks, grad_blocks, precision=highest) / blk_size
    )
    new_right = (
        0.5 * right_stats[0]
        + 0.5 * jnp.einsum("sji,sjk->sik", grad_blocks, grad_blocks, precision=highest) / blk_size
    )
    update_step = jnp.einsum("sij,sjk->sik", left_roots[0], grad_blocks, precision=highest)
    update_step = jnp.einsum("sij,sjk->sik", update_step, right_roots[0], precision=highest)
    new_masters = masters[0] - rate_matrix * update_step
    return (
        mixed,
        input_grad,
        grad_blocks[None],
        new_masters[None],
        new_left[None],
        new_right[None],
        new_vectors,
        new_momentum,
    )


def solution(mesh):
    return jax.shard_map(
        on_device,
        mesh=mesh,
        in_specs=(
            P("dp", None),
            P("dp", None),
            P("dp"),
            P(),
            P("tensor", "dp", None, None),
            P("tensor", "dp", None, None),
            P("tensor", "dp", None, None),
            P("tensor", "dp", None, None),
            P("tensor", "dp", None, None),
            P(),
            P(),
        ),
        out_specs=(
            P(("dp", "tensor"), None),
            P(("dp", "tensor"), None),
            P("tensor", "dp", None, None),
            P("tensor", "dp", None, None),
            P("tensor", "dp", None, None),
            P("tensor", "dp", None, None),
            P(),
            P(),
        ),
        check_vma=False,
    )
```

profile of v0, /device:TPU:0, one launch (start us, length us, event | category | flops | bytes accessed | tf_op | source)
XLA Modules:
  0.0 953.4 jit_solution(12270465933401899179)
XLA Ops:
  7.3 2.1 bitcast_convert_fusion
  15.7 2.4 convert_reduce_fusion.2
  18.0 2.9 multiply_reduce_fusion.8
  24.2 2.2 fusion.36
  28.0 88.9 %all-gather.2.cloned.1.call-done = bf16[224,128,128]{2,1,0:T(8,128)(2,1)} async-done(((bf16[14,128,128]{2,1,0:T(8,128)(2,1)}), bf16[224,128,128]{2,1,0:T(8,128)(2,1)}) %all-gather.2.cloned.1.call-update) | async-done | bytes 7340048 | tf_op jit(solution)/shard_map/all_gather | solution.py:103
  116.9 11.4 %gather_fusion = bf16[216,128,128]{2,1,0:T(8,128)(2,1)} fusion(bf16[224,128,128]{2,1,0:T(8,128)(2,1)} %all-gather.2.cloned.1.call-done, s32[1024]{0:T(1024)S(1)} %pad_clamp_fusion.1), kind=kCustom, calls=%fused_computation | custom fusion | bytes 14156640 | tf_op jit(solution)/shard_map/jit(_take)/gather | solution.py:104
  128.3 3.7 broadcast_select_fusion
  132.2 4.3 fusion.155
  136.5 2.8 copy.41
  139.3 6.8 fusion.159
  161.6 2.3 multiply_convert_fusion.4
  165.5 2.2 fusion.91
  167.7 3.3 copy.44
  171.0 3.5 copy.45
  175.3 3.4 fusion.162
  178.7 2.8 fusion.24
  181.6 4.0 fusion.99
  185.5 6.2 multiply_reduce_fusion.2
  191.7 2.8 fusion.78
  194.5 7.3 multiply_convert_fusion.2
  201.9 2.9 fusion.94
  206.2 8.4 fusion.161
  214.7 9.0 fusion.2
  223.7 10.5 %fusion.53 = f32[2048,6,64]{0,2,1:T(8,128)} fusion(f32[2048,6,64]{0,2,1:T(8,128)} %copy-done.8, bf16[512,6,64]{0,2,1:T(8,128)(2,1)S(1)} %bitcast.244, f32[6,512,1536]{2,1,0:T(8,128)} %get-tuple-element.177, f32[6,512]{1,0:T(8,128)S(1)} %log_add_fusion.1), kind=kOutput, calls=%fused_computation.109 | convolution fusion | flops 614006784 | bytes 23998464 | tf_op jit(solution)/shard_map/hqk,qhe->khe/dot_general | solution.py:254
  234.2 12.1 %multiply_reduce_fusion.1 = (f32[6,512]{1,0:T(8,128)S(1)}, f32[6,512,1536]{2,1,0:T(8,128)}) fusion(f32[6,512,1536]{2,1,0:T(8,128)} %get-tuple-element.177, f32[6,512]{1,0:T(8,128)S(1)} %log_add_fusion.1, bf16[512,6,64]{0,2,1:T(8,128)(2,1)S(1)} %bitcast.245, bf16[1536,6,64]{0,2,1:T(8,128)(2,1)S(1)} %bitcast.241), kind=kOutput, calls=%fused_computation.14 | convolution fusion | flops 618132480 | bytes 39346176 | tf_op jit(solution)/shard_map/qhe,khe->hqk/dot_general | solution.py:230
  246.3 12.9 %multiply_convert_fusion.1 = bf16[6,512,1536]{2,1,0:T(8,128)(2,1)S(1)} fusion(f32[6,512,1536]{2,1,0:T(8,128)} %get-tuple-element.187, f32[6,512,1536]{2,1,0:T(8,128)} %get-tuple-element.177, f32[6,512]{1,0:T(8,128)S(1)} %get-tuple-element.186, f32[6,512]{1,0:T(8,128)S(1)} %log_add_fusion.1), kind=kLoop, calls=%fused_computation.13 | loop fusion | flops 18874368 | bytes 47210496 | tf_op jit(solution)/shard_map/convert_element_type | solution.py:237
  259.2 3.8 fusion.93
  265.9 34.4 %fusion.6 = (bf16[2048,1536]{1,0:T(8,128)(2,1)S(1)}, f32[2048,1536]{1,0:T(8,128)}) fusion(f32[1536]{0:T(1024)S(1)} %copy-done.66, bf16[96,8,12,128]{3,2,1,0:T(8,128)(2,1)S(1)} %bitcast.253, bf16[2048,768]{1,0:T(8,128)(2,1)S(1)} %copy-done.2, f32[768]{0:T(1024)S(1)} %copy-done.70, f32[768]{0:T(1024)S(1)} %copy-done.65, f32[2048]{0:T(1024)S(1)} %add_rsqrt_fusion, ...), kind=kOutput, calls=%fused_computation.24 | convolution fusion | flops 5048893440 | bytes 24408064 | tf_op jit(solution)/shard_map/dot_general | solution.py:191
  300.4 13.2 %convert_reduce_fusion = (f32[1536]{0:T(1024)}, bf16[2048,1536]{1,0:T(8,128)(2,1)S(1)}) fusion(f32[2048,1536]{1,0:T(8,128)} %get-tuple-element.171, f32[1536]{0:T(1024)S(1)} %copy-done.66, bf16[2048,768]{1,0:T(8,128)(2,1)S(1)} %copy-done.19, bf16[192,8,6,128]{3,2,1,0:T(8,128)(2,1)S(1)} %bitcast.255), kind=kOutput, calls=%fused_computation.32 | convolution fusion | flops 4872731136 | bytes 24391680 | tf_op jit(solution)/shard_map/dot_general | solution.py:18
  313.6 7.0 fusion.60
  320.6 6.9 fusion.58
  327.5 10.7 %fusion.160 = (f32[6,512]{1,0:T(8,128)S(1)}, f32[6,512,2048]{2,1,0:T(8,128)}) fusion(bf16[2048,6,64]{0,2,1:T(8,128)(2,1)S(1)} %get-tuple-element.194, bf16[2048,6,64]{0,2,1:T(8,128)(2,1)S(1)} %copy-done.13, pred[512,2048]{1,0:T(8,128)(4,1)S(1)} %copy-done.17), kind=kOutput, calls=%fused_computation.283 | convolution fusion | flops 824177664 | bytes 28192768 | tf_op jit(solution)/shard_map/qhe,khe->hqk/dot_general | solution.py:159
  338.3 10.9 %fusion = f32[6,512]{1,0:T(8,128)S(1)} fusion(f32[6,512,2048]{2,1,0:T(8,128)} %get-tuple-element.175, f32[6,512]{1,0:T(8,128)S(1)} %get-tuple-element.174), kind=kLoop, calls=%fused_computation.9 | loop fusion | flops 12579840 | bytes 25190400 | tf_op jit(solution)/shard_map/reduce_sum | solution.py:179
  349.2 11.9 %fusion.39 = bf16[2048,6,64]{0,2,1:T(8,128)(2,1)} fusion(f32[2048,6,64]{0,2,1:T(8,128)S(1)} %copy-done.9, bf16[512,6,64]{0,2,1:T(8,128)(2,1)S(1)} %bitcast.242, f32[6,512,2048]{2,1,0:T(8,128)} %get-tuple-element.175, f32[6,512]{1,0:T(8,128)S(1)} %log_add_fusion), kind=kOutput, calls=%fused_computation.97 | convolution fusion | flops 819462144 | bytes 30289920 | tf_op jit(solution)/shard_map/hqk,qhe->khe/dot_general | solution.py:254
  361.1 19.5 %multiply_reduce_fusion = (f32[6,512]{1,0:T(8,128)S(1)}, f32[6,512,2048]{2,1,0:T(8,128)}) fusion(f32[6,512,2048]{2,1,0:T(8,128)} %get-tuple-element.175, f32[6,512]{1,0:T(8,128)S(1)} %log_add_fusion, bf16[512,6,64]{0,2,1:T(8,128)(2,1)S(1)} %bitcast.243, bf16[2048,6,64]{0,2,1:T(8,128)(2,1)S(1)} %bitcast.227), kind=kOutput, calls=%fused_computation.4 | convolution fusion | flops 824177664 | bytes 52322304 | tf_op jit(solution)/shard_map/qhe,khe->hqk/dot_general | solution.py:230
  380.6 16.9 %multiply_convert_fusion = bf16[6,512,2048]{2,1,0:T(8,128)(2,1)S(1)} fusion(f32[6,512,2048]{2,1,0:T(8,128)} %get-tuple-element.189, f32[6,512,2048]{2,1,0:T(8,128)} %get-tuple-element.175, f32[6,512]{1,0:T(8,128)S(1)} %get-tuple-element.188, f32[6,512]{1,0:T(8,128)S(1)} %log_add_fusion), kind=kLoop, calls=%fused_computation.3 | loop fusion | flops 25165824 | bytes 62939136 | tf_op jit(solution)/shard_map/convert_element_type | solution.py:237
  397.6 5.3 fusion.92
  402.9 4.5 bitcast_add_fusion.1
  412.1 11.4 %multiply_reduce_fusion.4 = (f32[768]{0:T(1024)S(1)}, f32[2048]{0:T(1024)S(1)}, f32[2048]{0:T(1024)S(1)}, f32[768]{0:T(1024)S(1)}, f32[768]{0:T(1024)S(1)}, /*in...) fusion(bf16[2048,768]{1,0:T(8,128)(2,1)S(1)} %copy-done.3, ...), kind=kOutput, calls=%fused_computation.67 | convolution fusion | flops 3664761856 | bytes 22284288 | tf_op jit(solution)/shard_map/dot_general | solution.py:18
  423.6 6.5 multiply_convert_fusion.3
  430.3 9.9 %fusion.100 = bf16[6,64,512]{2,1,0:T(8,128)(2,1)S(1)} fusion(bf16[1536,6,64]{0,2,1:T(8,128)(2,1)} %bitcast.240, f32[6,512,1536]{2,1,0:T(8,128)} %get-tuple-element.177, f32[6,512]{1,0:T(8,128)S(1)} %copy-done.59, f32[6,512]{1,0:T(8,128)S(1)} %copy-done.57), kind=kOutput, calls=%fused_computation.169 | convolution fusion | flops 618332160 | bytes 20471808 | tf_op jit(solution)/shard_map/hqk,khe->qhe/dot_general | solution.py:182
  440.2 10.7 %fusion.101 = bf16[6,64,512]{2,1,0:T(8,128)(2,1)S(1)} fusion(bf16[2048,6,64]{0,2,1:T(8,128)(2,1)S(1)} %bitcast.228, f32[6,512,2048]{2,1,0:T(8,128)} %get-tuple-element.175, f32[6,512]{1,0:T(8,128)S(1)} %fusion, f32[6,512]{1,0:T(8,128)S(1)} %get-tuple-element.174), kind=kOutput, calls=%fused_computation.170 | convolution fusion | flops 824377344 | bytes 27156480 | tf_op jit(solution)/shard_map/hqk,khe->qhe/dot_general | solution.py:182
  451.7 3.5 add_convert_fusion
  455.3 5.0 copy.52
  460.3 11.8 %fusion.153 = f32[768,1536]{1,0:T(8,128)} fusion(bf16[2048,1536]{1,0:T(8,128)(2,1)} %copy-done.74, bf16[2048,768]{1,0:T(8,128)(2,1)} %param.31, f32[768]{0:T(1024)S(1)} %copy-done.71, f32[768]{0:T(1024)S(1)} %copy-done.65, f32[2048]{0:T(1024)S(1)} %add_rsqrt_fusion, f32[2048]{0:T(1024)S(1)} %broadcast_multiply_fusion.4), kind=kOutput, calls=%fused_computation.276 | convolution fusion | flops 4841275392 | bytes 14178304 | tf_op jit(solution)/shard_map/dot_general | solution.py:18
  472.1 6.7 reshape.811
  478.8 6.7 copy.53
  485.4 8.7 fusion.165
  494.1 6.8 reshape.813
  501.0 5.9 copy.54
  506.9 6.1 fusion.152
  513.0 4.8 reshape.808
  517.8 5.5 copy.51
  524.7 4.1 fusion.164
  528.8 7.8 pad_maximum_fusion
  536.7 5.5 convert_element_type.106
  544.2 2.2 convert_reduce_fusion.1
  546.9 4.0 convert_reduce_fusion.3
  551.0 42.9 %psum.15 = f32[9984]{0:T(1024)S(1)} all-reduce(f32[9984]{0:T(1024)S(1)} %constant_dynamic-update-slice_fusion), channel_id=1, replica_groups=mesh['dp'=16,'tensor'=2] {'dp','tensor'}, use_global_device_ids=true, to_apply=%region_31.32 | all-reduce | flops 9984 | bytes 79872 | tf_op jit(solution)/shard_map/psum | solution.py:307
  593.9 4.1 add_convert_fusion.3
  598.7 329.6 %all-reduce.4.cloned.1.call-done = f32[216,128,128]{2,1,0:T(8,128)} async-done(((f32[216,128,128]{2,1,0:T(8,128)}), f32[216,128,128]{2,1,0:T(8,128)}) %all-reduce.4.cloned.1.call-update) | async-done | bytes 14155792 | tf_op jit(solution)/shard_map/psum | solution.py:322
  928.2 5.6 gather_fusion.1
  935.0 4.3 fusion.85
  939.3 4.0 fusion.83
  (267 shorter events, 47.5 us)
Async XLA Ops:
  7.2 936.1 %copy-start = (f32[1,14,128,128]{3,2,1,0:T(8,128)S(1)}, f32[1,14,128,128]{3,2,1,0:T(8,128)}, u32[]{:S(2)}) copy-start(f32[1,14,128,128]{3,2,1,0:T(8,128)} %param.38) | copy-start | bytes 2752516
  7.2 14.8 %slice-start.5 = ((s32[2048]{0:T(1024)}), s32[1024]{0:T(1024)S(1)}, s32[]{:S(2)}) async-start(s32[2048]{0:T(1024)} %param.33), calls=%async_computation.11 | async-start | bytes 8192 | tf_op jit(solution)/shard_map/slice | solution.py:167
  7.2 17.1 %copy-start.53 = (s32[2048]{0:T(1024)S(1)}, s32[2048]{0:T(1024)}, u32[]{:S(2)}) copy-start(s32[2048]{0:T(1024)} %param.33) | copy-start | bytes 24580
  7.2 13.9 %copy-start.54 = (f32[9984]{0:T(1024)S(1)}, f32[9984]{0:T(1024)}, u32[]{:S(2)}) copy-start(f32[9984]{0:T(1024)} %param.40) | copy-start | bytes 119812
  7.2 109.7 %all-gather.2.cloned.1.call-start = ((), (), s32[]{:S(2)}) async-start(), calls=%async_computation.2 | async-start | bytes 7798784 | tf_op jit(solution)/shard_map/all_gather | solution.py:103
  9.4 537.5 %reduce-scatter.5.cloned.1.call-start = ((), (), s32[]{:S(2)}) async-start(), calls=%async_computation.4 | async-start | bytes 4718592 | tf_op jit(solution)/shard_map/reduce_scatter | solution.py:277
  21.7 117.6 %copy-start.63 = (f32[768]{0:T(1024)}, f32[768]{0:T(1024)S(1)}, u32[]{:S(2)}) copy-start(f32[768]{0:T(1024)S(1)} %get-tuple-element.160) | copy-start | bytes 9220
  21.7 117.6 %copy-start.68 = (f32[768]{0:T(1024)}, f32[768]{0:T(1024)S(1)}, u32[]{:S(2)}) copy-start(f32[768]{0:T(1024)S(1)} %get-tuple-element.159) | copy-start | bytes 9220
  24.2 123.0 %copy-start.43 = (f32[2048,8]{0,1:T(8,128)}, f32[2048,8]{0,1:T(8,128)S(1)}, u32[]{:S(2)}) copy-start(f32[2048,8]{0,1:T(8,128)S(1)} %get-tuple-element.164) | copy-start | bytes 196612
  132.0 4.4 copy-start.10
  154.1 173.4 %copy-start.1 = (bf16[2048,6,64]{0,2,1:T(8,128)(2,1)}, bf16[2048,6,64]{0,2,1:T(8,128)(2,1)S(1)}, u32[]{:S(2)}) copy-start(bf16[2048,6,64]{0,2,1:T(8,128)(2,1)S(1)} %get-tuple-element.194) | copy-start | bytes 4718596
  164.0 7.1 copy-start.15
  167.7 6.8 copy-start.36
  171.0 4.3 copy-start.42
  194.5 7.4 copy-start.8
  206.2 8.5 copy-start.5
  214.7 9.0 copy-start.56
  223.7 10.5 %copy-start.58 = (f32[6,512]{1,0:T(8,128)}, f32[6,512]{1,0:T(8,128)S(1)}, u32[]{:S(2)}) copy-start(f32[6,512]{1,0:T(8,128)S(1)} %fusion.2) | copy-start | bytes 36868
  223.7 10.5 %copy-start.29 = (bf16[1536,384]{0,1:T(8,128)(2,1)S(1)}, bf16[1536,384]{0,1:T(8,128)(2,1)}, u32[]{:S(2)}) copy-start(bf16[1536,384]{0,1:T(8,128)(2,1)} %slice.511) | copy-start | bytes 3538948
  264.9 35.5 %copy-start.7 = (f32[2048,6,64]{0,2,1:T(8,128)}, f32[2048,6,64]{0,2,1:T(8,128)S(1)}, u32[]{:S(2)}) copy-start(f32[2048,6,64]{0,2,1:T(8,128)S(1)} %fusion.46) | copy-start | bytes 9437188
  265.9 34.5 %copy-start.19 = (bf16[2048,768]{1,0:T(8,128)(2,1)S(1)}, bf16[2048,768]{1,0:T(8,128)(2,1)}, u32[]{:S(2)}) copy-start(bf16[2048,768]{1,0:T(8,128)(2,1)} %param.32) | copy-start | bytes 9437188
  265.9 34.5 %copy-start.38 = (bf16[12,6,128,128]{3,1,2,0:T(8,128)(2,1)S(1)}, bf16[12,6,128,128]{3,1,2,0:T(8,128)(2,1)}, u32[]{:S(2)}) copy-start(bf16[12,6,128,128]{3,1,2,0:T(8,128)(2,1)} %copy.45) | copy-start | bytes 7077892
  300.4 20.2 %copy-start.73 = (bf16[2048,1536]{1,0:T(8,128)(2,1)}, bf16[2048,1536]{1,0:T(8,128)(2,1)S(1)}, u32[]{:S(2)}) copy-start(bf16[2048,1536]{1,0:T(8,128)(2,1)S(1)} %get-tuple-element.170) | copy-start | bytes 18874372
  313.6 7.0 copy-start.74
  320.6 6.9 copy-start.17
  338.3 10.9 %copy-start.9 = (f32[2048,6,64]{0,2,1:T(8,128)S(1)}, f32[2048,6,64]{0,2,1:T(8,128)}, u32[]{:S(2)}) copy-start(f32[2048,6,64]{0,2,1:T(8,128)} %fusion.53) | copy-start | bytes 9437188
  338.3 10.9 %copy-start.31 = (bf16[512,384]{0,1:T(8,128)(2,1)S(1)}, bf16[512,384]{0,1:T(8,128)(2,1)}, u32[]{:S(2)}) copy-start(bf16[512,384]{0,1:T(8,128)(2,1)} %get-tuple-element.150) | copy-start | bytes 1179652
  349.2 12.0 %copy-start.21 = (bf16[2048,384]{0,1:T(8,128)(2,1)S(1)}, bf16[2048,384]{0,1:T(8,128)(2,1)}, u32[]{:S(2)}) copy-start(bf16[2048,384]{0,1:T(8,128)(2,1)} %slice.514) | copy-start | bytes 4718596
  402.9 4.7 copy-start.35
  402.9 4.7 copy-start.39
  402.9 4.7 copy-start.40
  407.9 4.2 copy-start.41
  407.9 4.2 copy-start.64
  408.5 15.1 %slice-start.3 = ((s8[6291456]{0:T(1024)(128)(4,1)}), s8[4194304]{0:T(1024)(128)(4,1)S(1)}, s32[]{:S(2)}) async-start(s8[6291456]{0:T(1024)(128)(4,1)} %bitcast.232), calls=%async_computation.9 | async-start | bytes 8388608
  408.6 14.9 %copy-start.25 = (bf16[2048,6,64]{0,2,1:T(8,128)(2,1)}, bf16[2048,6,64]{0,2,1:T(8,128)(2,1)S(1)}, u32[]{:S(2)}) copy-start(bf16[2048,6,64]{0,2,1:T(8,128)(2,1)S(1)} %pad_maximum_fusion.4) | copy-start | bytes 4718596
  408.8 14.7 %copy-start.27 = (bf16[2048,6,64]{0,2,1:T(8,128)(2,1)}, bf16[2048,6,64]{0,2,1:T(8,128)(2,1)S(1)}, u32[]{:S(2)}) copy-start(bf16[2048,6,64]{0,2,1:T(8,128)(2,1)S(1)} %pad_maximum_fusion.5) | copy-start | bytes 4718596
  412.1 11.4 %slice-start.4 = ((s8[6291456]{0:T(1024)(128)(4,1)}), s8[2097152]{0:T(1024)(128)(4,1)S(1)}, s32[]{:S(2)}) async-start(s8[6291456]{0:T(1024)(128)(4,1)} %bitcast.232), calls=%async_computation.10 | async-start | bytes 4194304
  423.6 6.7 copy-start.57
  423.6 6.7 copy-start.59
  430.2 10.0 %copy-start.22 = (bf16[2048,384]{0,1:T(8,128)(2,1)S(1)}, bf16[2048,384]{0,1:T(8,128)(2,1)}, u32[]{:S(2)}) copy-start(bf16[2048,384]{0,1:T(8,128)(2,1)} %slice.514) | copy-start | bytes 4718596
  430.2 163.7 %reduce-scatter.3.cloned.1.call-start = ((), (), s32[]{:S(2)}) async-start(), calls=%async_computation.3 | async-start | bytes 4718592 | tf_op jit(solution)/shard_map/reduce_scatter | solution.py:198
  430.2 21.4 %slice-start.6 = ((s8[6291456]{0:T(1024)(128)(4,1)}), s8[4194304]{0:T(1024)(128)(4,1)S(1)}, s32[]{:S(2)}) async-start(s8[6291456]{0:T(1024)(128)(4,1)} %bitcast.274), calls=%async_computation.12 | async-start | bytes 8388608
  440.1 10.8 %copy-start.50 = (bf16[6,64,512]{2,1,0:T(8,128)(2,1)}, bf16[6,64,512]{2,1,0:T(8,128)(2,1)S(1)}, u32[]{:S(2)}) copy-start(bf16[6,64,512]{2,1,0:T(8,128)(2,1)S(1)} %fusion.100) | copy-start | bytes 1179652
  440.2 11.5 %copy-start.47 = (bf16[3,6,128,128]{3,1,2,0:T(8,128)(2,1)S(1)}, bf16[3,6,128,128]{3,1,2,0:T(8,128)(2,1)}, u32[]{:S(2)}) copy-start(bf16[3,6,128,128]{3,1,2,0:T(8,128)(2,1)} %copy-done.46) | copy-start | bytes 1769476
  440.2 11.5 %copy-start.48 = (bf16[6,64,512]{2,1,0:T(8,128)(2,1)S(1)}, bf16[6,64,512]{2,1,0:T(8,128)(2,1)}, u32[]{:S(2)}) copy-start(bf16[6,64,512]{2,1,0:T(8,128)(2,1)} %fusion.98) | copy-start | bytes 1179652
  440.2 11.5 %copy-start.49 = (bf16[6,64,512]{2,1,0:T(8,128)(2,1)S(1)}, bf16[6,64,512]{2,1,0:T(8,128)(2,1)}, u32[]{:S(2)}) copy-start(bf16[6,64,512]{2,1,0:T(8,128)(2,1)} %fusion.99) | copy-start | bytes 1179652
  440.2 11.5 %slice-start.7 = ((s8[6291456]{0:T(1024)(128)(4,1)}), s8[2097152]{0:T(1024)(128)(4,1)S(1)}, s32[]{:S(2)}) async-start(s8[6291456]{0:T(1024)(128)(4,1)} %bitcast.274), calls=%async_computation.13 | async-start | bytes 4194304
  455.3 5.0 copy-start.71
  455.3 472.9 %all-reduce.4.cloned.1.call-start = ((), (), s32[]{:S(2)}) async-start(), calls=%async_computation.5 | async-start | bytes 28311552 | tf_op jit(solution)/shard_map/psum | solution.py:322
  478.8 6.7 copy-start.20
  500.9 5.9 copy-start.4
  500.9 5.9 copy-start.24
  501.0 5.9 copy-start.26
  501.0 5.9 copy-start.28
  501.0 5.9 copy-start.69
  523.2 5.6 slice-start.1
  523.2 5.6 copy-start.14
  536.7 7.2 copy-start.67
  542.3 51.6 %copy-start.61 = (f32[768]{0:T(1024)S(1)}, f32[768]{0:T(1024)}, u32[]{:S(2)}) copy-start(f32[768]{0:T(1024)} %get-tuple-element.156) | copy-start | bytes 9220
  542.3 51.7 %copy-start.62 = (f32[768]{0:T(1024)S(1)}, f32[768]{0:T(1024)}, u32[]{:S(2)}) copy-start(f32[768]{0:T(1024)} %get-tuple-element.161) | copy-start | bytes 9220
  546.9 51.1 %copy-start.55 = (f32[9984]{0:T(1024)S(1)}, f32[9984]{0:T(1024)}, u32[]{:S(2)}) copy-start(f32[9984]{0:T(1024)} %param.40) | copy-start | bytes 119812
  546.9 51.1 %copy-start.60 = (f32[9984]{0:T(1024)S(1)}, f32[9984]{0:T(1024)}, u32[]{:S(2)}) copy-start(f32[9984]{0:T(1024)} %param.41) | copy-start | bytes 119812
  598.0 346.4 %copy-start.30 = (f32[1,14,128,128]{3,2,1,0:T(8,128)S(1)}, f32[1,14,128,128]{3,2,1,0:T(8,128)}, u32[]{:S(2)}) copy-start(f32[1,14,128,128]{3,2,1,0:T(8,128)} %param.35) | copy-start | bytes 2752516
  933.8 10.6 %copy-start.45 = (f32[1,14,128,128]{3,2,1,0:T(8,128)S(1)}, f32[1,14,128,128]{3,2,1,0:T(8,128)}, u32[]{:S(2)}) copy-start(f32[1,14,128,128]{3,2,1,0:T(8,128)} %param.39) | copy-start | bytes 2752516
  (23 other events, 61.3 us)
Sparse Core Ops, SparseCore 0:
  11.3 105.5 all-gather.1
  430.3 9.4 reduce-scatter.4
  455.4 9.4 reduce-scatter.2
  536.8 391.3 all-reduce.3
where the time goes:
time: 962 us; the launch traced here: 953 us
  waiting for transfers between devices  419 us (44%)
  matrix products  267 us (28%)
  other arithmetic  119 us (12%)
  local copies, waits for them, and re-layouts  90.4 us (9%)
  blocking collectives  42.9 us (4%)
  between operations  15.6 us (2%)
    psum x1, waiting for transfers between devices, on_device(): summed = lax.psum(local_blocks, 'dp')  330 us
    all_gather x1, waiting for transfers between devices, on_device(): gathered = lax.all_gather(copies, 'dp', axis=0, tiled=True)  88.9 us
    dot_general x8, matrix products, contract(): lax.dot_general(first_op, second_op, (((first_dim,), (second_dim,)), ((),...  63.7 us
    psum x1, blocking collectives, on_device(): vector_sum = lax.psum(jnp.concatenate(pieces), ('dp', 'tensor'))  42.9 us
    convert_element_type x4, other arithmetic, on_device(): grad_scores = (prob_full * (grad_probs - row_delta)).astype(jnp.bfloat16)  39.5 us
    dot_general x4, matrix products, on_device(): jnp.einsum('qhe,khe->hqk', grad_attended[row_low:row_high], values_all[:r...  39.1 us
    dot_general x1, matrix products, on_device(): jnp.dot(norm_two, w_in, preferred_element_type=jnp.float32) + bias_in  34.4 us
    dot_general x4, matrix products, on_device(): jnp.einsum('hqk,qhe->khe', prob_low, grad_attended[row_low:row_high], pre...  27.2 us
  transfers between devices with their start and end apart: 4, of which 2 were waited for; matrix products, arithmetic and copies ran while one was open for 15% of the time, Pallas kernels for 0%

commit v1 on v0

--- a/solution.py
+++ b/solution.py
@@ -304,7 +304,7 @@
         ),
         bias_grad_out,
     ]
-    vector_sum = lax.psum(jnp.concatenate(pieces), ("dp", "tensor"))
+    vector_sum = jnp.sum(lax.all_gather(jnp.concatenate(pieces), ("dp", "tensor")), axis=0)
     grad_scale = 1.0 / jnp.sqrt(jnp.float32(data_ways * tok_rows))
     vector_grad = vector_sum * grad_scale
     new_momentum = decay_vector * vector_momentum + (1.0 - decay_vector) * vector_grad

time: 962 us -> 998 us (1.037)
  waiting for transfers between devices: 419 us -> 494 us
  blocking collectives: 42.9 us -> 0 us
    psum x1, waiting for transfers between devices: 330 us -> 394 us  [on_device(): summed = lax.psum(local_blocks, 'dp')]
    psum x1 -> x0, blocking collectives: 42.9 us -> none  [on_device(): vector_sum = lax.psum(jnp.concatenate(pieces), ('dp', 'tensor'))]
    all_gather x0 -> x1, waiting for transfers between devices: none -> 10.7 us  [on_device(): lax.all_gather(jnp.concatenate(pieces), ('dp', 'tensor'))]
  transfers between devices with their start and end apart: 4 -> 5, of which waited for: 2 -> 3; matrix products, arithmetic and copies ran while one was open for 15% -> 15% of each run, Pallas kernels for 0% -> 0%
where the time goes in v1:
time: 998 us; the launch traced here: 990 us
  waiting for transfers between devices  494 us (49%)
  matrix products  269 us (27%)
  other arithmetic  119 us (12%)
  local copies, waits for them, and re-layouts  91.8 us (9%)
  between operations  15.6 us (2%)
    psum x1, waiting for transfers between devices, on_device(): summed = lax.psum(local_blocks, 'dp')  394 us
    all_gather x1, waiting for transfers between devices, on_device(): gathered = lax.all_gather(copies, 'dp', axis=0, tiled=True)  88.8 us
    dot_general x8, matrix products, contract(): lax.dot_general(first_op, second_op, (((first_dim,), (second_dim,)), ((),...  65.9 us
    convert_element_type x4, other arithmetic, on_device(): grad_scores = (prob_full * (grad_probs - row_delta)).astype(jnp.bfloat16)  39.5 us
    dot_general x4, matrix products, on_device(): jnp.einsum('qhe,khe->hqk', grad_attended[row_low:row_high], values_all[:r...  39.2 us
    dot_general x1, matrix products, on_device(): jnp.dot(norm_two, w_in, preferred_element_type=jnp.float32) + bias_in  34.4 us
    dot_general x4, matrix products, on_device(): jnp.einsum('hqk,qhe->khe', prob_low, grad_attended[row_low:row_high], pre...  27.2 us
    dot_general x4, matrix products, on_device(): jnp.einsum('hqk,khe->qhe', weights_low, values_all[:key_span], preferred_...  26.5 us
  transfers between devices with their start and end apart: 5, of which 3 were waited for; matrix products, arithmetic and copies ran while one was open for 15% of the time, Pallas kernels for 0%

profile of v1, /device:TPU:0, one launch (start us, length us, event | category | flops | bytes accessed | tf_op | source)
XLA Modules:
  0.0 989.6 jit_solution(14693523701086706311)
XLA Ops:
  7.3 2.1 bitcast_convert_fusion
  15.7 2.4 convert_reduce_fusion.2
  18.1 2.9 multiply_reduce_fusion.8
  24.3 2.2 fusion.36
  28.1 88.8 %all-gather.5.cloned.1.call-done = bf16[224,128,128]{2,1,0:T(8,128)(2,1)} async-done(((bf16[14,128,128]{2,1,0:T(8,128)(2,1)}), bf16[224,128,128]{2,1,0:T(8,128)(2,1)}) %all-gather.5.cloned.1.call-update) | async-done | bytes 7340048 | tf_op jit(solution)/shard_map/all_gather | solution.py:103
  116.9 11.4 %gather_fusion = bf16[216,128,128]{2,1,0:T(8,128)(2,1)} fusion(bf16[224,128,128]{2,1,0:T(8,128)(2,1)} %all-gather.5.cloned.1.call-done, s32[1024]{0:T(1024)S(1)} %pad_clamp_fusion.1), kind=kCustom, calls=%fused_computation | custom fusion | bytes 14156640 | tf_op jit(solution)/shard_map/jit(_take)/gather | solution.py:104
  128.3 3.7 broadcast_select_fusion
  132.2 4.3 fusion.155
  136.5 2.8 copy.41
  139.3 6.8 fusion.159
  161.6 2.3 multiply_convert_fusion.4
  165.5 2.2 fusion.91
  167.7 3.3 copy.44
  171.0 3.5 copy.45
  175.3 3.4 fusion.162
  178.7 2.8 fusion.24
  181.6 4.0 fusion.99
  185.5 6.2 multiply_reduce_fusion.2
  191.7 2.8 fusion.78
  194.5 7.3 multiply_convert_fusion.2
  201.9 2.9 fusion.94
  206.2 8.3 fusion.161
  214.5 9.0 fusion.2
  223.6 10.5 %fusion.53 = f32[2048,6,64]{0,2,1:T(8,128)} fusion(f32[2048,6,64]{0,2,1:T(8,128)} %copy-done.7, bf16[512,6,64]{0,2,1:T(8,128)(2,1)S(1)} %bitcast.244, f32[6,512,1536]{2,1,0:T(8,128)} %get-tuple-element.177, f32[6,512]{1,0:T(8,128)S(1)} %log_add_fusion.1), kind=kOutput, calls=%fused_computation.109 | convolution fusion | flops 614006784 | bytes 23998464 | tf_op jit(solution)/shard_map/hqk,qhe->khe/dot_general | solution.py:254
  234.1 12.1 %multiply_reduce_fusion.1 = (f32[6,512]{1,0:T(8,128)S(1)}, f32[6,512,1536]{2,1,0:T(8,128)}) fusion(f32[6,512,1536]{2,1,0:T(8,128)} %get-tuple-element.177, f32[6,512]{1,0:T(8,128)S(1)} %log_add_fusion.1, bf16[512,6,64]{0,2,1:T(8,128)(2,1)S(1)} %bitcast.245, bf16[1536,6,64]{0,2,1:T(8,128)(2,1)S(1)} %bitcast.241), kind=kOutput, calls=%fused_computation.14 | convolution fusion | flops 618132480 | bytes 39346176 | tf_op jit(solution)/shard_map/qhe,khe->hqk/dot_general | solution.py:230
  246.2 12.9 %multiply_convert_fusion.1 = bf16[6,512,1536]{2,1,0:T(8,128)(2,1)S(1)} fusion(f32[6,512,1536]{2,1,0:T(8,128)} %get-tuple-element.187, f32[6,512,1536]{2,1,0:T(8,128)} %get-tuple-element.177, f32[6,512]{1,0:T(8,128)S(1)} %get-tuple-element.186, f32[6,512]{1,0:T(8,128)S(1)} %log_add_fusion.1), kind=kLoop, calls=%fused_computation.13 | loop fusion | flops 18874368 | bytes 47210496 | tf_op jit(solution)/shard_map/convert_element_type | solution.py:237
  259.1 3.8 fusion.93
  265.9 34.4 %fusion.6 = (bf16[2048,1536]{1,0:T(8,128)(2,1)S(1)}, f32[2048,1536]{1,0:T(8,128)}) fusion(f32[1536]{0:T(1024)S(1)} %copy-done.65, bf16[96,8,12,128]{3,2,1,0:T(8,128)(2,1)S(1)} %bitcast.253, bf16[2048,768]{1,0:T(8,128)(2,1)S(1)} %copy-done.2, f32[768]{0:T(1024)S(1)} %copy-done.69, f32[768]{0:T(1024)S(1)} %copy-done.64, f32[2048]{0:T(1024)S(1)} %add_rsqrt_fusion, ...), kind=kOutput, calls=%fused_computation.24 | convolution fusion | flops 5048893440 | bytes 24408064 | tf_op jit(solution)/shard_map/dot_general | solution.py:191
  300.3 13.2 %convert_reduce_fusion = (f32[1536]{0:T(1024)}, bf16[2048,1536]{1,0:T(8,128)(2,1)S(1)}) fusion(f32[2048,1536]{1,0:T(8,128)} %get-tuple-element.171, f32[1536]{0:T(1024)S(1)} %copy-done.65, bf16[2048,768]{1,0:T(8,128)(2,1)S(1)} %copy-done.18, bf16[192,8,6,128]{3,2,1,0:T(8,128)(2,1)S(1)} %bitcast.255), kind=kOutput, calls=%fused_computation.32 | convolution fusion | flops 4872731136 | bytes 24391680 | tf_op jit(solution)/shard_map/dot_general | solution.py:18
  313.6 7.0 fusion.60
  320.6 6.9 fusion.58
  327.5 10.7 %fusion.160 = (f32[6,512]{1,0:T(8,128)S(1)}, f32[6,512,2048]{2,1,0:T(8,128)}) fusion(bf16[2048,6,64]{0,2,1:T(8,128)(2,1)S(1)} %get-tuple-element.194, bf16[2048,6,64]{0,2,1:T(8,128)(2,1)S(1)} %copy-done.12, pred[512,2048]{1,0:T(8,128)(4,1)S(1)} %copy-done.16), kind=kOutput, calls=%fused_computation.283 | convolution fusion | flops 824177664 | bytes 28192768 | tf_op jit(solution)/shard_map/qhe,khe->hqk/dot_general | solution.py:159
  338.2 10.9 %fusion = f32[6,512]{1,0:T(8,128)S(1)} fusion(f32[6,512,2048]{2,1,0:T(8,128)} %get-tuple-element.175, f32[6,512]{1,0:T(8,128)S(1)} %get-tuple-element.174), kind=kLoop, calls=%fused_computation.9 | loop fusion | flops 12579840 | bytes 25190400 | tf_op jit(solution)/shard_map/reduce_sum | solution.py:179
  349.1 11.9 %fusion.39 = bf16[2048,6,64]{0,2,1:T(8,128)(2,1)} fusion(f32[2048,6,64]{0,2,1:T(8,128)S(1)} %copy-done.8, bf16[512,6,64]{0,2,1:T(8,128)(2,1)S(1)} %bitcast.242, f32[6,512,2048]{2,1,0:T(8,128)} %get-tuple-element.175, f32[6,512]{1,0:T(8,128)S(1)} %log_add_fusion), kind=kOutput, calls=%fused_computation.97 | convolution fusion | flops 819462144 | bytes 30289920 | tf_op jit(solution)/shard_map/hqk,qhe->khe/dot_general | solution.py:254
  361.1 19.5 %multiply_reduce_fusion = (f32[6,512]{1,0:T(8,128)S(1)}, f32[6,512,2048]{2,1,0:T(8,128)}) fusion(f32[6,512,2048]{2,1,0:T(8,128)} %get-tuple-element.175, f32[6,512]{1,0:T(8,128)S(1)} %log_add_fusion, bf16[512,6,64]{0,2,1:T(8,128)(2,1)S(1)} %bitcast.243, bf16[2048,6,64]{0,2,1:T(8,128)(2,1)S(1)} %bitcast.227), kind=kOutput, calls=%fused_computation.4 | convolution fusion | flops 824177664 | bytes 52322304 | tf_op jit(solution)/shard_map/qhe,khe->hqk/dot_general | solution.py:230
  380.6 16.9 %multiply_convert_fusion = bf16[6,512,2048]{2,1,0:T(8,128)(2,1)S(1)} fusion(f32[6,512,2048]{2,1,0:T(8,128)} %get-tuple-element.189, f32[6,512,2048]{2,1,0:T(8,128)} %get-tuple-element.175, f32[6,512]{1,0:T(8,128)S(1)} %get-tuple-element.188, f32[6,512]{1,0:T(8,128)S(1)} %log_add_fusion), kind=kLoop, calls=%fused_computation.3 | loop fusion | flops 25165824 | bytes 62939136 | tf_op jit(solution)/shard_map/convert_element_type | solution.py:237
  397.5 5.3 fusion.92
  402.9 4.5 bitcast_add_fusion.1
  412.1 11.4 %multiply_reduce_fusion.4 = (f32[768]{0:T(1024)S(1)}, f32[2048]{0:T(1024)S(1)}, f32[2048]{0:T(1024)S(1)}, f32[768]{0:T(1024)S(1)}, f32[768]{0:T(1024)S(1)}, /*in...) fusion(bf16[2048,768]{1,0:T(8,128)(2,1)S(1)} %copy-done.3, ...), kind=kOutput, calls=%fused_computation.67 | convolution fusion | flops 3664761856 | bytes 22284288 | tf_op jit(solution)/shard_map/dot_general | solution.py:18
  423.5 6.5 multiply_convert_fusion.3
  430.2 9.9 fusion.100
  440.1 10.7 %fusion.101 = bf16[6,64,512]{2,1,0:T(8,128)(2,1)S(1)} fusion(bf16[2048,6,64]{0,2,1:T(8,128)(2,1)S(1)} %bitcast.228, f32[6,512,2048]{2,1,0:T(8,128)} %get-tuple-element.175, f32[6,512]{1,0:T(8,128)S(1)} %fusion, f32[6,512]{1,0:T(8,128)S(1)} %get-tuple-element.174), kind=kOutput, calls=%fused_computation.170 | convolution fusion | flops 824377344 | bytes 27156480 | tf_op jit(solution)/shard_map/hqk,khe->qhe/dot_general | solution.py:182
  451.7 3.5 add_convert_fusion
  455.3 5.0 copy.52
  460.2 11.8 %fusion.153 = f32[768,1536]{1,0:T(8,128)} fusion(bf16[2048,1536]{1,0:T(8,128)(2,1)} %copy-done.73, bf16[2048,768]{1,0:T(8,128)(2,1)} %param.31, f32[768]{0:T(1024)S(1)} %copy-done.70, f32[768]{0:T(1024)S(1)} %copy-done.64, f32[2048]{0:T(1024)S(1)} %add_rsqrt_fusion, f32[2048]{0:T(1024)S(1)} %broadcast_multiply_fusion.4), kind=kOutput, calls=%fused_computation.276 | convolution fusion | flops 4841275392 | bytes 14178304 | tf_op jit(solution)/shard_map/dot_general | solution.py:18
  472.1 6.7 reshape.811
  478.7 6.7 copy.53
  485.4 8.7 fusion.165
  494.1 6.6 reshape.813
  500.7 5.9 copy.54
  506.9 2.2 convert_reduce_fusion.1
  509.8 4.0 convert_reduce_fusion.3
  514.5 8.8 fusion.152
  523.3 4.9 reshape.808
  528.2 5.5 copy.51
  533.9 3.7 fusion.164
  538.0 7.8 pad_maximum_fusion
  545.9 5.0 convert_element_type.106
  552.8 4.2 add_convert_fusion.3
  557.0 10.7 %all-gather.7.cloned.1.call-done = f32[32,1,9984]{2,1,0:T(1,128)} async-done(((f32[1,1,9984]{2,1,0:T(1,128)}), f32[32,1,9984]{2,1,0:T(1,128)}) %all-gather.7.cloned.1.call-update) | async-done | bytes 1277968 | tf_op jit(solution)/shard_map/all_gather | solution.py:307
  570.4 394.0 %all-reduce.4.cloned.1.call-done = f32[216,128,128]{2,1,0:T(8,128)} async-done(((f32[216,128,128]{2,1,0:T(8,128)}), f32[216,128,128]{2,1,0:T(8,128)}) %all-reduce.4.cloned.1.call-update) | async-done | bytes 14155792 | tf_op jit(solution)/shard_map/psum | solution.py:322
  964.4 5.6 gather_fusion.1
  971.2 4.3 fusion.85
  975.5 4.0 fusion.83
  (269 shorter events, 49.8 us)
Async XLA Ops:
  7.2 972.3 %copy-start = (f32[1,14,128,128]{3,2,1,0:T(8,128)S(1)}, f32[1,14,128,128]{3,2,1,0:T(8,128)}, u32[]{:S(2)}) copy-start(f32[1,14,128,128]{3,2,1,0:T(8,128)} %param.38) | copy-start | bytes 2752516
  7.2 14.9 %slice-start.5 = ((s32[2048]{0:T(1024)}), s32[1024]{0:T(1024)S(1)}, s32[]{:S(2)}) async-start(s32[2048]{0:T(1024)} %param.33), calls=%async_computation.12 | async-start | bytes 8192 | tf_op jit(solution)/shard_map/slice | solution.py:167
  7.2 17.1 %copy-start.52 = (s32[2048]{0:T(1024)S(1)}, s32[2048]{0:T(1024)}, u32[]{:S(2)}) copy-start(s32[2048]{0:T(1024)} %param.33) | copy-start | bytes 24580
  7.2 13.9 %copy-start.53 = (f32[9984]{0:T(1024)S(1)}, f32[9984]{0:T(1024)}, u32[]{:S(2)}) copy-start(f32[9984]{0:T(1024)} %param.40) | copy-start | bytes 119812
  7.2 109.7 %all-gather.5.cloned.1.call-start = ((), (), s32[]{:S(2)}) async-start(), calls=%async_computation.2 | async-start | bytes 7798784 | tf_op jit(solution)/shard_map/all_gather | solution.py:103
  9.4 500.4 %reduce-scatter.5.cloned.1.call-start = ((), (), s32[]{:S(2)}) async-start(), calls=%async_computation.4 | async-start | bytes 4718592 | tf_op jit(solution)/shard_map/reduce_scatter | solution.py:277
  21.8 117.6 %copy-start.62 = (f32[768]{0:T(1024)}, f32[768]{0:T(1024)S(1)}, u32[]{:S(2)}) copy-start(f32[768]{0:T(1024)S(1)} %get-tuple-element.160) | copy-start | bytes 9220
  21.8 117.6 %copy-start.67 = (f32[768]{0:T(1024)}, f32[768]{0:T(1024)S(1)}, u32[]{:S(2)}) copy-start(f32[768]{0:T(1024)S(1)} %get-tuple-element.159) | copy-start | bytes 9220
  24.3 122.9 %copy-start.40 = (f32[2048,8]{0,1:T(8,128)}, f32[2048,8]{0,1:T(8,128)S(1)}, u32[]{:S(2)}) copy-start(f32[2048,8]{0,1:T(8,128)S(1)} %get-tuple-element.164) | copy-start | bytes 196612
  132.1 4.4 copy-start.9
  154.2 173.3 %copy-start.1 = (bf16[2048,6,64]{0,2,1:T(8,128)(2,1)}, bf16[2048,6,64]{0,2,1:T(8,128)(2,1)S(1)}, u32[]{:S(2)}) copy-start(bf16[2048,6,64]{0,2,1:T(8,128)(2,1)S(1)} %get-tuple-element.194) | copy-start | bytes 4718596
  164.0 7.1 copy-start.14
  167.7 6.8 copy-start.33
  171.0 4.3 copy-start.39
  194.5 7.4 copy-start.7
  206.2 8.3 copy-start.4
  214.5 9.0 copy-start.55
  223.5 10.6 %copy-start.57 = (f32[6,512]{1,0:T(8,128)}, f32[6,512]{1,0:T(8,128)S(1)}, u32[]{:S(2)}) copy-start(f32[6,512]{1,0:T(8,128)S(1)} %fusion.2) | copy-start | bytes 36868
  223.6 10.5 %copy-start.26 = (bf16[1536,384]{0,1:T(8,128)(2,1)S(1)}, bf16[1536,384]{0,1:T(8,128)(2,1)}, u32[]{:S(2)}) copy-start(bf16[1536,384]{0,1:T(8,128)(2,1)} %slice.511) | copy-start | bytes 3538948
  264.8 35.5 %copy-start.6 = (f32[2048,6,64]{0,2,1:T(8,128)}, f32[2048,6,64]{0,2,1:T(8,128)S(1)}, u32[]{:S(2)}) copy-start(f32[2048,6,64]{0,2,1:T(8,128)S(1)} %fusion.46) | copy-start | bytes 9437188
  265.8 34.5 %copy-start.18 = (bf16[2048,768]{1,0:T(8,128)(2,1)S(1)}, bf16[2048,768]{1,0:T(8,128)(2,1)}, u32[]{:S(2)}) copy-start(bf16[2048,768]{1,0:T(8,128)(2,1)} %param.32) | copy-start | bytes 9437188
  265.8 34.5 %copy-start.35 = (bf16[12,6,128,128]{3,1,2,0:T(8,128)(2,1)S(1)}, bf16[12,6,128,128]{3,1,2,0:T(8,128)(2,1)}, u32[]{:S(2)}) copy-start(bf16[12,6,128,128]{3,1,2,0:T(8,128)(2,1)} %copy.45) | copy-start | bytes 7077892
  300.3 20.2 %copy-start.72 = (bf16[2048,1536]{1,0:T(8,128)(2,1)}, bf16[2048,1536]{1,0:T(8,128)(2,1)S(1)}, u32[]{:S(2)}) copy-start(bf16[2048,1536]{1,0:T(8,128)(2,1)S(1)} %get-tuple-element.170) | copy-start | bytes 18874372
  313.6 7.0 copy-start.73
  320.6 6.9 copy-start.16
  338.2 10.9 %copy-start.8 = (f32[2048,6,64]{0,2,1:T(8,128)S(1)}, f32[2048,6,64]{0,2,1:T(8,128)}, u32[]{:S(2)}) copy-start(f32[2048,6,64]{0,2,1:T(8,128)} %fusion.53) | copy-start | bytes 9437188
  338.2 10.9 %copy-start.28 = (bf16[512,384]{0,1:T(8,128)(2,1)S(1)}, bf16[512,384]{0,1:T(8,128)(2,1)}, u32[]{:S(2)}) copy-start(bf16[512,384]{0,1:T(8,128)(2,1)} %get-tuple-element.150) | copy-start | bytes 1179652
  349.1 12.0 %copy-start.20 = (bf16[2048,384]{0,1:T(8,128)(2,1)S(1)}, bf16[2048,384]{0,1:T(8,128)(2,1)}, u32[]{:S(2)}) copy-start(bf16[2048,384]{0,1:T(8,128)(2,1)} %slice.514) | copy-start | bytes 4718596
  402.8 4.7 copy-start.32
  402.8 4.7 copy-start.36
  402.9 4.7 copy-start.37
  407.8 4.2 copy-start.38
  407.8 4.2 copy-start.63
  408.4 15.1 %slice-start.3 = ((s8[6291456]{0:T(1024)(128)(4,1)}), s8[4194304]{0:T(1024)(128)(4,1)S(1)}, s32[]{:S(2)}) async-start(s8[6291456]{0:T(1024)(128)(4,1)} %bitcast.232), calls=%async_computation.10 | async-start | bytes 8388608
  408.6 14.8 %copy-start.24 = (bf16[2048,6,64]{0,2,1:T(8,128)(2,1)}, bf16[2048,6,64]{0,2,1:T(8,128)(2,1)S(1)}, u32[]{:S(2)}) copy-start(bf16[2048,6,64]{0,2,1:T(8,128)(2,1)S(1)} %pad_maximum_fusion.4) | copy-start | bytes 4718596
  408.8 14.7 %copy-start.25 = (bf16[2048,6,64]{0,2,1:T(8,128)(2,1)}, bf16[2048,6,64]{0,2,1:T(8,128)(2,1)S(1)}, u32[]{:S(2)}) copy-start(bf16[2048,6,64]{0,2,1:T(8,128)(2,1)S(1)} %pad_maximum_fusion.5) | copy-start | bytes 4718596
  412.1 11.4 %slice-start.4 = ((s8[6291456]{0:T(1024)(128)(4,1)}), s8[2097152]{0:T(1024)(128)(4,1)S(1)}, s32[]{:S(2)}) async-start(s8[6291456]{0:T(1024)(128)(4,1)} %bitcast.232), calls=%async_computation.11 | async-start | bytes 4194304
  423.5 6.7 copy-start.56
  423.5 6.7 copy-start.58
  430.1 10.0 %copy-start.21 = (bf16[2048,384]{0,1:T(8,128)(2,1)S(1)}, bf16[2048,384]{0,1:T(8,128)(2,1)}, u32[]{:S(2)}) copy-start(bf16[2048,384]{0,1:T(8,128)(2,1)} %slice.514) | copy-start | bytes 4718596
  430.1 122.6 %reduce-scatter.3.cloned.1.call-start = ((), (), s32[]{:S(2)}) async-start(), calls=%async_computation.3 | async-start | bytes 4718592 | tf_op jit(solution)/shard_map/reduce_scatter | solution.py:198
  430.2 21.4 %slice-start.6 = ((s8[6291456]{0:T(1024)(128)(4,1)}), s8[4194304]{0:T(1024)(128)(4,1)S(1)}, s32[]{:S(2)}) async-start(s8[6291456]{0:T(1024)(128)(4,1)} %bitcast.274), calls=%async_computation.13 | async-start | bytes 8388608
  440.1 10.8 %copy-start.47 = (bf16[6,64,512]{2,1,0:T(8,128)(2,1)}, bf16[6,64,512]{2,1,0:T(8,128)(2,1)S(1)}, u32[]{:S(2)}) copy-start(bf16[6,64,512]{2,1,0:T(8,128)(2,1)S(1)} %fusion.100) | copy-start | bytes 1179652
  440.1 11.5 %copy-start.44 = (bf16[3,6,128,128]{3,1,2,0:T(8,128)(2,1)S(1)}, bf16[3,6,128,128]{3,1,2,0:T(8,128)(2,1)}, u32[]{:S(2)}) copy-start(bf16[3,6,128,128]{3,1,2,0:T(8,128)(2,1)} %copy-done.43) | copy-start | bytes 1769476
  440.1 11.5 %copy-start.45 = (bf16[6,64,512]{2,1,0:T(8,128)(2,1)S(1)}, bf16[6,64,512]{2,1,0:T(8,128)(2,1)}, u32[]{:S(2)}) copy-start(bf16[6,64,512]{2,1,0:T(8,128)(2,1)} %fusion.98) | copy-start | bytes 1179652
  440.1 11.5 %copy-start.46 = (bf16[6,64,512]{2,1,0:T(8,128)(2,1)S(1)}, bf16[6,64,512]{2,1,0:T(8,128)(2,1)}, u32[]{:S(2)}) copy-start(bf16[6,64,512]{2,1,0:T(8,128)(2,1)} %fusion.99) | copy-start | bytes 1179652
  440.1 11.5 %slice-start.7 = ((s8[6291456]{0:T(1024)(128)(4,1)}), s8[2097152]{0:T(1024)(128)(4,1)S(1)}, s32[]{:S(2)}) async-start(s8[6291456]{0:T(1024)(128)(4,1)} %bitcast.274), calls=%async_computation.14 | async-start | bytes 4194304
  455.2 5.1 copy-start.70
  455.2 112.5 %all-gather.7.cloned.1.call-start = ((), (), s32[]{:S(2)}) async-start(), calls=%async_computation.6 | async-start | bytes 1317888 | tf_op jit(solution)/shard_map/all_gather | solution.py:307
  478.7 6.7 copy-start.19
  500.7 5.9 copy-start.66
  500.7 6.2 copy-start.23
  506.6 8.0 copy-start.68
  514.5 449.9 %all-reduce.4.cloned.1.call-start = ((), (), s32[]{:S(2)}) async-start(), calls=%async_computation.5 | async-start | bytes 28311552 | tf_op jit(solution)/shard_map/psum | solution.py:322
  523.3 10.4 %copy-start.48 = (bf16[6,64,512]{2,1,0:T(8,128)(2,1)S(1)}, bf16[6,64,512]{2,1,0:T(8,128)(2,1)}, u32[]{:S(2)}) copy-start(bf16[6,64,512]{2,1,0:T(8,128)(2,1)} %copy-done.47) | copy-start | bytes 1179652
  523.3 10.4 %copy-start.50 = (bf16[6,64,512]{2,1,0:T(8,128)(2,1)S(1)}, bf16[6,64,512]{2,1,0:T(8,128)(2,1)}, u32[]{:S(2)}) copy-start(bf16[6,64,512]{2,1,0:T(8,128)(2,1)} %copy-done.49) | copy-start | bytes 1179652
  533.7 4.2 slice-start.1
  533.7 4.2 copy-start.13
  545.9 6.9 copy-start.60
  545.9 6.9 copy-start.61
  545.9 23.8 %copy-start.54 = (f32[9984]{0:T(1024)S(1)}, f32[9984]{0:T(1024)}, u32[]{:S(2)}) copy-start(f32[9984]{0:T(1024)} %param.40) | copy-start | bytes 119812
  545.9 23.8 %copy-start.59 = (f32[9984]{0:T(1024)S(1)}, f32[9984]{0:T(1024)}, u32[]{:S(2)}) copy-start(f32[9984]{0:T(1024)} %param.41) | copy-start | bytes 119812
  569.8 410.8 %copy-start.27 = (f32[1,14,128,128]{3,2,1,0:T(8,128)S(1)}, f32[1,14,128,128]{3,2,1,0:T(8,128)}, u32[]{:S(2)}) copy-start(f32[1,14,128,128]{3,2,1,0:T(8,128)} %param.35) | copy-start | bytes 2752516
  970.0 10.6 %copy-start.42 = (f32[1,14,128,128]{3,2,1,0:T(8,128)S(1)}, f32[1,14,128,128]{3,2,1,0:T(8,128)}, u32[]{:S(2)}) copy-start(f32[1,14,128,128]{3,2,1,0:T(8,128)} %param.39) | copy-start | bytes 2752516
  (23 other events, 61.3 us)
Sparse Core Ops, SparseCore 0:
  11.3 105.5 all-gather.4
  430.2 9.4 reduce-scatter.4
  455.3 9.4 reduce-scatter.2
  514.6 53.0 all-gather.6
  574.0 390.3 all-reduce.3
